TPU v7x, 32 devices: a whole 2x2x4 slice. The times are simulated.
32 devices in a mesh: groups: 2 (over y), docs: 8 (over z, x), help: 2 (over core).
Axes of the slice: x: 2, y: 2, z: 4, core: 2. Of those that a mesh axis runs over, the one named last changes fastest.
Arguments:
- token_states: bfloat16 [4096, 2, 1024], P(('groups', 'docs', 'help')), parts along dimension 0, may hold values from -6 to 6
- lengths: int32 [4096], P(('groups', 'docs', 'help')), parts along dimension 0, may hold values from 1 to 2
- cluster_id: int32 [4096], P(('groups', 'docs', 'help')), parts along dimension 0, may hold values from 0 to 7, as said below
- proj_weight: bfloat16 [1024, 1024], replicated, may hold values from -0.1875 to 0.1875
- proj_bias: float32 [1024], replicated, may hold values from -4 to 4
Outputs:
- max_sim: float32 [4096], P(('groups', 'docs', 'help')), parts along dimension 0
There are 2 independent parts, one for each index of `groups`. A program takes and returns all parts, laid end to end along the dimension named above; an argument that names none is the same for every part. Nothing has to cross between parts.
Inputs may be any that keep to these rules, and one draw needn't show every extreme that they name: `cluster_id`: clusters 1 * k to 1 * k + 1 - 1 form owner k. Among the 128 documents of one device (aligned blocks of the document dimension), at most 32 belong to one owner, and in every draw one owner gets exactly 32 documents from every device.
All inputs are finite; a program needn't handle non-finite values.
Results may differ from a plain program's by a relative error of at most 0.0003.
Values may be sent and summed in bfloat16 or wider, within the bound.
A program may use at most 64 MiB of HBM per device.

v0:
```python
import functools

import jax
import jax.numpy as jnp
from jax import lax
from jax.experimental import pallas as pl
from jax.experimental.pallas import tpu as pltpu
from jax.sharding import PartitionSpec as P

CL_OWN = 1


def partner(value, axis, bit):
    return lax.ppermute(value, axis, [(i, i ^ 1 << bit) for i in range(lax.axis_size(axis))])


def slot_maxima(own_emb, own_ids, self_pos, col_emb, col_ids):
    row_total = own_emb.shape[0]
    block = min(row_total, 512)
    col_pos = lax.broadcasted_iota(jnp.int32, (col_emb.shape[0],), 0)

    def block_max(pieces):
        part_emb, part_ids, part_self = pieces
        duplicate_scores = jnp.einsum(
            "rd,cd->rc", part_emb, col_emb, preferred_element_type=jnp.float32
        )
        match = (
            (part_ids[:, None] == col_ids[None, :])
            & (col_ids[None, :] >= 0)
            & (part_self[:, None] != col_pos[None, :])
        )
        return jnp.max(jnp.where(match, duplicate_scores, -1.0), axis=1)

    steps_count = row_total // block
    result = lax.map(
        block_max,
        (
            own_emb.reshape(steps_count, block, own_emb.shape[1]),
            own_ids.reshape(steps_count, block),
            self_pos.reshape(steps_count, block),
        ),
    )
    return result.reshape(row_total)


def body(token_states, lengths, cluster_id, proj_weight, proj_bias):
    row_count, seq_len, feat_dim = token_states.shape
    owners = lax.axis_size("docs")
    slot_cap = 2 * row_count // owners
    position_count = owners * slot_cap
    token_mask = (
        lax.broadcasted_iota(jnp.int32, (row_count, seq_len), 1) < lengths[:, None]
    ).astype(jnp.bfloat16)
    summed = jnp.einsum("rsd,rs->rd", token_states, token_mask, preferred_element_type=jnp.float32)
    pooled = (summed / lengths[:, None].astype(jnp.float32)).astype(jnp.bfloat16)
    hidden = jnp.tanh(jnp.dot(pooled, proj_weight, preferred_element_type=jnp.float32) + proj_bias)
    factor = lax.rsqrt(jnp.sum(hidden * hidden, axis=1, keepdims=True) + 1e-06)
    embedded = (hidden * factor).astype(jnp.bfloat16)
    dest_owner = cluster_id // CL_OWN
    same_owner = dest_owner[:, None] == dest_owner[None, :]
    earlier = lax.broadcasted_iota(jnp.int32, (row_count, row_count), 1) < lax.broadcasted_iota(
        jnp.int32, (row_count, row_count), 0
    )
    slot_rank = jnp.sum((same_owner & earlier).astype(jnp.int32), axis=1)
    target = dest_owner * slot_cap + slot_rank
    chooser = lax.broadcasted_iota(jnp.int32, (position_count, row_count), 0) == target[None, :]
    packed = jnp.dot(
        chooser.astype(jnp.bfloat16), embedded, preferred_element_type=jnp.float32
    ).astype(jnp.bfloat16)
    packed_ids = jnp.max(jnp.where(chooser, cluster_id[None, :], -1), axis=1)
    own_emb, own_ids = (
        lax.all_to_all(packed, "docs", split_axis=0, concat_axis=0, tiled=True),
        lax.all_to_all(packed_ids, "docs", split_axis=0, concat_axis=0, tiled=True),
    )
    mate_emb, mate_ids = partner((own_emb, own_ids), "help", 0)
    col_emb = jnp.concatenate([own_emb, mate_emb], axis=0)
    col_ids = jnp.concatenate([own_ids, mate_ids], axis=0)
    self_pos = lax.broadcasted_iota(jnp.int32, (position_count,), 0)
    maxima = slot_maxima(own_emb, own_ids, self_pos, col_emb, col_ids)
    returned = lax.all_to_all(maxima, "docs", split_axis=0, concat_axis=0, tiled=True)
    return jnp.max(jnp.where(chooser, returned[:, None], -3.0), axis=0)


EMPTY = 2.0
DIRECT_LIMIT = 16


def flipped(index, step):
    bit = 1
    while bit <= step:
        if step & bit:
            index = index + bit * (1 - 2 * ((index // bit) % 2))
        bit *= 2
    return index


def fused_kernel(
    owners,
    slot_cap,
    states_hbm,
    lengths_hbm,
    ids_hbm,
    weight_hbm,
    bias_hbm,
    out_ref,
    lengths_ref,
    ids_ref,
    bias_ref,
    states_ref,
    weight_ref,
    packed_ref,
    own_ref,
    maxima_ref,
    returned_ref,
    small_sem,
    states_sem,
    weight_sem,
    pack_send,
    pack_recv,
    back_send,
    back_recv,
    onward_sem,
):
    me = lax.axis_index("docs")
    side = lax.axis_index("help")
    row_count, seq_len, feat_dim = states_ref.shape
    quarter = owners // 4
    half = owners // 2
    sources = 2 * owners
    late = 2 * 3 * quarter
    group = row_count // slot_cap
    my_half = me // half
    near = me + my_half * (owners - 1 - 2 * me)
    outer = 1 - near // quarter
    is_owner = near >= quarter

    small_copies = [
        pltpu.make_async_copy(source, held, small_sem.at[position])
        for position, (source, held) in enumerate(
            [(ids_hbm, ids_ref), (lengths_hbm, lengths_ref), (bias_hbm, bias_ref)]
        )
    ]
    for copy in small_copies:
        copy.start()
    states_copy = pltpu.make_async_copy(states_hbm, states_ref, states_sem)
    states_copy.start()
    weight_copy = pltpu.make_async_copy(weight_hbm, weight_ref, weight_sem)
    weight_copy.start()
    barrier = pltpu.get_barrier_semaphore()
    peers = [(step, flip) for step in range(owners - 1, -1, -1) for flip in (0, 1) if step + flip]

    def peer_id(step, flip):
        return {"docs": flipped(me, step), "help": flipped(side, flip)}

    inner = [(spot, spot_side) for spot in range(quarter, half) for spot_side in (0, 1)]

    def greet(semaphore):
        def signal(spot, spot_side):
            docs = spot + my_half * (owners - 1 - 2 * spot)
            pl.semaphore_signal(
                semaphore,
                inc=1,
                device_id={"docs": docs, "help": spot_side},
                device_id_type=pl.DeviceIdType.MESH,
            )

        @pl.when(is_owner)
        def _():
            for spot, spot_side in inner:
                signal(owners - 1 - spot, spot_side)
                signal(spot - quarter, spot_side)

        @pl.when(jnp.logical_not(is_owner))
        def _():
            for spot, spot_side in inner:
                signal(spot, spot_side)

    def await_greetings(semaphore):
        pl.semaphore_wait(semaphore, len(inner) * (2 - outer))

    greet(barrier)

    for copy in small_copies:
        copy.wait()
    ids = ids_ref[...]
    across = jnp.broadcast_to(ids, (row_count, row_count))
    down = jnp.transpose(across)
    earlier = lax.broadcasted_iota(jnp.int32, (row_count, row_count), 0) < lax.broadcasted_iota(
        jnp.int32, (row_count, row_count), 1
    )
    rank = jnp.sum(jnp.where((across == down) & earlier, 1, 0), axis=0, keepdims=True)
    dest = ids // CL_OWN

    counts = jnp.transpose(
        jnp.broadcast_to(lengths_ref[...].astype(jnp.float32), (row_count, row_count))
    )[:, 0:1]
    states_copy.wait()
    states = states_ref[...]
    summed = states[:, 0, :].astype(jnp.float32)
    for position in range(1, seq_len):
        token = states[:, position, :].astype(jnp.float32)
        summed = summed + jnp.where(counts > position, token, 0.0)
    pooled = (summed / counts).astype(jnp.bfloat16)

    weight_copy.wait()
    hidden = jnp.tanh(
        jnp.dot(pooled, weight_ref[...], preferred_element_type=jnp.float32) + bias_ref[...]
    )
    factor = lax.rsqrt(jnp.sum(hidden * hidden, axis=1, keepdims=True) + 1e-06)
    embedded = (hidden * factor).astype(jnp.bfloat16)

    def turn_target(turn):
        spot = quarter + (turn // 2 + (1 - outer) * quarter) % half
        spot_side = turn % 2
        docs = spot + my_half * (owners - 1 - 2 * spot)
        number = (docs - quarter) * 2 + spot_side
        crosses = spot // half
        slot = (near + crosses * (owners - 1 - 2 * near)) * 2 + side
        return docs, spot_side, number, slot

    def pack(number):
        slots = lax.broadcasted_iota(jnp.int32, (slot_cap, row_count), 0)
        chooser = jnp.where((slots == rank) & (dest == number), 1.0, 0.0)
        filled = jnp.sum(chooser, axis=1, keepdims=True)
        rows = jnp.dot(
            chooser.astype(jnp.bfloat16), embedded, preferred_element_type=jnp.float32
        )
        return jnp.where(filled > 0.5, rows, EMPTY).astype(jnp.bfloat16)

    def to_owner(turn):
        docs, spot_side, _, slot = turn_target(turn)
        return pltpu.make_async_remote_copy(
            src_ref=packed_ref.at[turn],
            dst_ref=own_ref.at[slot],
            send_sem=pack_send.at[turn],
            recv_sem=pack_recv.at[slot],
            device_id={"docs": docs, "help": spot_side},
            device_id_type=pl.DeviceIdType.MESH,
        )

    def from_source(slot):
        return pltpu.make_async_remote_copy(
            src_ref=packed_ref.at[0],
            dst_ref=own_ref.at[slot],
            send_sem=pack_send.at[0],
            recv_sem=pack_recv.at[slot],
            device_id=peer_id(0, 1),
            device_id_type=pl.DeviceIdType.MESH,
        )

    my_number = (me - quarter) * 2 + side
    my_slot = near * 2 + side

    def back(number, position):
        where = peer_id(*peers[position])
        slot = (where["docs"] + my_half * (owners - 1 - 2 * where["docs"])) * 2 + where["help"]
        return pltpu.make_async_remote_copy(
            src_ref=maxima_ref.at[slot // group],
            dst_ref=returned_ref.at[number],
            send_sem=back_send.at[position],
            recv_sem=back_recv.at[number],
            device_id=where,
            device_id_type=pl.DeviceIdType.MESH,
        )

    for turn in range(owners):
        docs, spot_side, number, slot = turn_target(turn)
        remote = (docs != me) | (side != spot_side)
        packed_ref[turn] = pack(number)
        if turn == 0:
            await_greetings(barrier)
            greet(onward_sem)
        if turn == half:
            await_greetings(onward_sem)

        @pl.when(remote)
        def _():
            to_owner(turn).start()

        @pl.when(jnp.logical_not(remote))
        def _():
            own_ref[slot] = packed_ref[turn]

    def column_max(columns, rows, same):
        scores = lax.dot_general(
            columns, rows, (((1,), (1,)), ((), ())), preferred_element_type=jnp.float32
        )
        keep = columns[:, 0:1].astype(jnp.float32) < 1.5
        if same:
            keep = keep & (
                lax.broadcasted_iota(jnp.int32, scores.shape, 0)
                != lax.broadcasted_iota(jnp.int32, scores.shape, 1)
            )
        return jnp.max(jnp.where(keep, scores, -1.0), axis=0, keepdims=True)

    @pl.when(is_owner)
    def _():
        for slot in range(late):

            @pl.when(my_slot != slot)
            def _():
                from_source(slot).wait_recv()

        first = own_ref[:late].reshape(late * slot_cap, feat_dim)
        first_max = column_max(first, first, True)
        for slot in range(late, sources):
            from_source(slot).wait_recv()
        last = own_ref[late:].reshape((sources - late) * slot_cap, feat_dim)
        maxima = jnp.concatenate(
            [
                jnp.maximum(first_max, column_max(last, first, False)),
                jnp.maximum(column_max(first, last, False), column_max(last, last, True)),
            ],
            axis=1,
        )
        for part in range(sources // group):
            maxima_ref[part] = maxima[:, part * row_count : (part + 1) * row_count]
        for position in range(len(peers)):
            back(my_number, position).start()
        returned_ref[my_number] = maxima_ref[my_slot // group]

    owner_half = (dest // 2 + quarter) // half
    my_slots = jnp.where(owner_half == my_half, near, owners - 1 - near) * 2 + side
    finder = jnp.where(
        lax.broadcasted_iota(jnp.int32, (row_count, row_count), 0)
        == my_slots % group * slot_cap + rank,
        1.0,
        0.0,
    ).astype(jnp.bfloat16)
    for number in range(owners):

        @pl.when((my_number != number) | jnp.logical_not(is_owner))
        def _():
            back(number, 0).wait_recv()

    exact = jnp.concatenate([returned_ref[number] for number in range(owners)], axis=0)
    parts = []
    for _ in range(3):
        part = exact.astype(jnp.bfloat16)
        parts.append(part.astype(jnp.float32))
        exact = exact - parts[-1]
    picked = jnp.dot(
        jnp.concatenate(parts, axis=0).astype(jnp.bfloat16),
        finder,
        preferred_element_type=jnp.float32,
    )
    picked = picked[:owners] + (picked[owners : 2 * owners] + picked[2 * owners :])
    mine = lax.broadcasted_iota(jnp.int32, picked.shape, 0) == dest
    out_ref[...] = jnp.sum(jnp.where(mine, picked, 0.0), axis=0, keepdims=True)
    for turn in range(owners):
        docs, spot_side, _, _ = turn_target(turn)

        @pl.when((docs != me) | (side != spot_side))
        def _():
            to_owner(turn).wait_send()

    @pl.when(is_owner)
    def _():
        for position in range(len(peers)):
            back(my_number, position).wait_send()


def fused_body(token_states, lengths, cluster_id, proj_weight, proj_bias):
    row_count, seq_len, feat_dim = token_states.shape
    owners = lax.axis_size("docs")
    slot_cap = 2 * row_count // owners
    vmem = pl.BlockSpec(memory_space=pltpu.VMEM)
    hbm = pl.BlockSpec(memory_space=pl.ANY)
    sources = 2 * owners
    result = pl.pallas_call(
        functools.partial(fused_kernel, owners, slot_cap),
        out_shape=pltpu.VMEM((1, row_count), jnp.float32),
        in_specs=[hbm] * 5,
        out_specs=vmem,
        scratch_shapes=[
            pltpu.VMEM((1, row_count), jnp.int32),
            pltpu.VMEM((1, row_count), jnp.int32),
            pltpu.VMEM((1, feat_dim), jnp.float32),
            pltpu.VMEM(token_states.shape, jnp.bfloat16),
            pltpu.VMEM(proj_weight.shape, jnp.bfloat16),
            pltpu.VMEM((owners, slot_cap, feat_dim), jnp.bfloat16),
            pltpu.VMEM((sources, slot_cap, feat_dim), jnp.bfloat16),
            pltpu.VMEM((sources * slot_cap // row_count, 1, row_count), jnp.float32),
            pltpu.VMEM((owners, 1, row_count), jnp.float32),
            pltpu.SemaphoreType.DMA((3,)),
            pltpu.SemaphoreType.DMA,
            pltpu.SemaphoreType.DMA,
            pltpu.SemaphoreType.DMA((owners,)),
            pltpu.SemaphoreType.DMA((sources,)),
            pltpu.SemaphoreType.DMA((sources,)),
            pltpu.SemaphoreType.DMA((owners,)),
            pltpu.SemaphoreType.REGULAR,
        ],
        compiler_params=pltpu.CompilerParams(collective_id=0, has_side_effects=True),
        name="scores",
    )(token_states, lengths[None, :], cluster_id[None, :], proj_weight, proj_bias[None, :])
    return result.reshape(row_count)


def solution(mesh):
    in_specs = (
        P(("groups", "docs", "help"), None, None),
        P(("groups", "docs", "help")),
        P(("groups", "docs", "help")),
        P(),
        P(),
    )
    out_specs = P(("groups", "docs", "help"))
    owners = mesh.shape["docs"]
    direct = 8 <= owners <= DIRECT_LIMIT and owners & (owners - 1) == 0 and mesh.shape["help"] == 2
    return jax.shard_map(fused_body if direct else body, mesh=mesh, in_specs=in_specs, out_specs=out_specs, check_vma=False)
```

profile of v0, /device:TPU:0, one launch (start us, length us, event | category | flops | bytes accessed | tf_op | source)
XLA Modules:
  0.0 23.8 jit_solution(9779230562354723585)
XLA Ops:
  0.0 23.3 %scores.1 = f32[1,128]{1,0:T(1,128)S(1)} custom-call(bf16[128,2,1024]{2,1,0:T(2,128)(2,1)} %states_hbm.1, s32[1,128]{1,0:T(1,128)} %bitcast.6, s32[1,128]{1,0:T(1,128)} %bitcast.7, bf16[1024,1024]{1,0:T(8,128)(2,1)} %weight_hbm.1, f32[1,1024]{1,0:T(1,128)} %bitcast.5), custom_call_target="tpu_custom_call" | custom-call | tf_op jit(solution)/shard_map/scores/pallas_call | solution.py:370
  23.3 0.5 %copy.7 = f32[128]{0:T(128)} copy(f32[128]{0:T(128)S(1)} %bitcast.4) | data formatting | bytes 1024
where the time goes:
time: 24 us; the launch traced here: 23.8 us
  Pallas kernels  23.3 us (97%)
  local copies, waits for them, and re-layouts  0.51 us (2%)
    pallas_call x1, Pallas kernels, fused_body(): pl.pallas_call(functools.partial(fused_kernel, owners, slot_cap), out_sha...  23.3 us
    unnamed x1, local copies, waits for them, and re-layouts  0.51 us

commit v1 on v0

v1 whole, which is shorter than its diff:
```python
import jax
import jax.numpy as jnp
from jax import lax
from jax.experimental import pallas as pl
from jax.experimental.pallas import tpu as pltpu
from jax.sharding import PartitionSpec as P

CL_OWN = 1


def partner(value, axis, bit):
    return lax.ppermute(value, axis, [(i, i ^ 1 << bit) for i in range(lax.axis_size(axis))])


def slot_maxima(own_emb, own_ids, self_pos, col_emb, col_ids):
    row_total = own_emb.shape[0]
    block = min(row_total, 512)
    col_pos = lax.broadcasted_iota(jnp.int32, (col_emb.shape[0],), 0)

    def block_max(pieces):
        part_emb, part_ids, part_self = pieces
        duplicate_scores = jnp.einsum(
            "rd,cd->rc", part_emb, col_emb, preferred_element_type=jnp.float32
        )
        match = (
            (part_ids[:, None] == col_ids[None, :])
            & (col_ids[None, :] >= 0)
            & (part_self[:, None] != col_pos[None, :])
        )
        return jnp.max(jnp.where(match, duplicate_scores, -1.0), axis=1)

    steps_count = row_total // block
    result = lax.map(
        block_max,
        (
            own_emb.reshape(steps_count, block, own_emb.shape[1]),
            own_ids.reshape(steps_count, block),
            self_pos.reshape(steps_count, block),
        ),
    )
    return result.reshape(row_total)


def body(token_states, lengths, cluster_id, proj_weight, proj_bias):
    row_count, seq_len, feat_dim = token_states.shape
    owners = lax.axis_size("docs")
    slot_cap = 2 * row_count // owners
    position_count = owners * slot_cap
    token_mask = (
        lax.broadcasted_iota(jnp.int32, (row_count, seq_len), 1) < lengths[:, None]
    ).astype(jnp.bfloat16)
    summed = jnp.einsum("rsd,rs->rd", token_states, token_mask, preferred_element_type=jnp.float32)
    pooled = (summed / lengths[:, None].astype(jnp.float32)).astype(jnp.bfloat16)
    hidden = jnp.tanh(jnp.dot(pooled, proj_weight, preferred_element_type=jnp.float32) + proj_bias)
    factor = lax.rsqrt(jnp.sum(hidden * hidden, axis=1, keepdims=True) + 1e-06)
    embedded = (hidden * factor).astype(jnp.bfloat16)
    dest_owner = cluster_id // CL_OWN
    same_owner = dest_owner[:, None] == dest_owner[None, :]
    earlier = lax.broadcasted_iota(jnp.int32, (row_count, row_count), 1) < lax.broadcasted_iota(
        jnp.int32, (row_count, row_count), 0
    )
    slot_rank = jnp.sum((same_owner & earlier).astype(jnp.int32), axis=1)
    target = dest_owner * slot_cap + slot_rank
    chooser = lax.broadcasted_iota(jnp.int32, (position_count, row_count), 0) == target[None, :]
    packed = jnp.dot(
        chooser.astype(jnp.bfloat16), embedded, preferred_element_type=jnp.float32
    ).astype(jnp.bfloat16)
    packed_ids = jnp.max(jnp.where(chooser, cluster_id[None, :], -1), axis=1)
    own_emb, own_ids = (
        lax.all_to_all(packed, "docs", split_axis=0, concat_axis=0, tiled=True),
        lax.all_to_all(packed_ids, "docs", split_axis=0, concat_axis=0, tiled=True),
    )
    mate_emb, mate_ids = partner((own_emb, own_ids), "help", 0)
    col_emb = jnp.concatenate([own_emb, mate_emb], axis=0)
    col_ids = jnp.concatenate([own_ids, mate_ids], axis=0)
    self_pos = lax.broadcasted_iota(jnp.int32, (position_count,), 0)
    maxima = slot_maxima(own_emb, own_ids, self_pos, col_emb, col_ids)
    returned = lax.all_to_all(maxima, "docs", split_axis=0, concat_axis=0, tiled=True)
    return jnp.max(jnp.where(chooser, returned[:, None], -3.0), axis=0)


ROWS = 4
CORES = 2
CHUNKS = 4
SAME = 4.0
SIBLING, CORNER, NEAR_TOO, END_TOO, AFTER = range(5)
ACROSS, OUTER, NEAR, END = (AFTER + 1 + CHUNKS * at for at in range(4))
FLOWS = END + CHUNKS


def meet_kernel(
    states_hbm,
    lengths_hbm,
    ids_hbm,
    weight_hbm,
    bias_hbm,
    out_ref,
    lengths_ref,
    bias_ref,
    states_ref,
    weight_ref,
    ids_ref,
    blocks_ref,
    marks_ref,
    detour_ref,
    best_ref,
    folded_ref,
    given_ref,
    taken_ref,
    small_sem,
    states_sem,
    weight_sem,
    block_send,
    block_recv,
    detour_recv,
    ids_send,
    ids_recv,
    best_send,
    best_recv,
):
    row_count, seq_len, feat_dim = states_ref.shape
    lines = blocks_ref.shape[0]
    columns = lines // CORES
    chunk = row_count // CHUNKS
    hub = ROWS - 2
    group = lax.axis_index("groups")
    docs = lax.axis_index("docs")
    core = lax.axis_index("help")
    depth = docs // columns
    col = docs % columns
    row = depth + group * (ROWS - 1 - 2 * depth)
    far_col = columns - 1 - col
    far_core = CORES - 1 - core
    line = col * CORES + core
    sibling_line = col * CORES + far_core
    across_line = far_col * CORES + core

    def device(at_row, at_col, at_core):
        at_depth = at_row + group * (ROWS - 1 - 2 * at_row)
        return {"docs": at_depth * columns + at_col, "help": at_core}

    def other_plane(at_row):
        at_depth = at_row + group * (ROWS - 1 - 2 * at_row)
        return {"groups": 1 - group, "docs": at_depth * columns + col, "help": core}

    def spot(at_line, at_row):
        return at_line * ROWS + at_row

    me = spot(line, row)
    sibling_device = device(row, col, far_core)

    small_copies = [
        pltpu.make_async_copy(source, held, small_sem.at[position])
        for position, (source, held) in enumerate(
            [(lengths_hbm, lengths_ref), (ids_hbm, ids_ref.at[me]), (bias_hbm, bias_ref)]
        )
    ]
    for copy in small_copies:
        copy.start()
    states_copy = pltpu.make_async_copy(states_hbm, states_ref, states_sem)
    states_copy.start()
    weight_copy = pltpu.make_async_copy(weight_hbm, weight_ref, weight_sem)
    weight_copy.start()

    barrier = pltpu.get_barrier_semaphore()

    def greet(*wheres):
        for where in wheres:
            pl.semaphore_signal(
                barrier, inc=1, device_id=where, device_id_type=pl.DeviceIdType.MESH
            )

    around = (core == 1) & ((row == 1) | (row == hub))

    def each_to(act):
        @pl.when(row < hub)
        def _():
            for at_core in range(CORES):
                act(device(hub, col, at_core))

        @pl.when(row == 1)
        def _():
            act(device(0, far_col, core))

        @pl.when(row > hub)
        def _():
            act(device(hub, col, core))
            act(device(hub, far_col, core))

        act(device(row, far_col, core))
        act(sibling_device)

    each_to(lambda where: greet(where))

    @pl.when(row == 0)
    def _():
        greet(device(1, col, core), device(1, far_col, core))

    @pl.when(row == 1)
    def _():
        greet(device(0, col, core))

    @pl.when(row == hub)
    def _():
        for at_row in range(hub):
            for at_core in range(CORES):
                greet(device(at_row, col, at_core))
        greet(device(hub + 1, col, core), device(hub + 1, far_col, core))

    @pl.when(around)
    def _():
        greet(other_plane(row))

        @pl.when(row == hub)
        def _():
            greet(other_plane(hub - 1))

    greetings = (
        2
        + 4 * (row < hub)
        + 6 * (row == hub)
        + 2 * (row > hub)
        + around * (1 + (row == hub))
    )

    def send(flow, part, at_line, at_row, where, lane=0):
        rows = blocks_ref.at[at_line, at_row, pl.ds(part * chunk, chunk)]
        pltpu.make_async_remote_copy(
            src_ref=rows,
            dst_ref=rows,
            send_sem=block_send.at[lane],
            recv_sem=block_recv.at[flow if flow <= AFTER else flow + part],
            device_id=where,
            device_id_type=pl.DeviceIdType.MESH,
        ).start()

    def waiter(held, send_sem, recv_sem):
        return pltpu.make_async_remote_copy(
            src_ref=held,
            dst_ref=held,
            send_sem=send_sem,
            recv_sem=recv_sem,
            device_id=sibling_device,
            device_id_type=pl.DeviceIdType.MESH,
        )

    def sent(lane, count):
        waiter(
            blocks_ref.at[0, pl.ds(0, count)], block_send.at[lane], block_recv.at[0]
        ).wait_send()

    def arrive(flow, part, at_line, at_row):
        rows = blocks_ref.at[at_line, at_row, pl.ds(part * chunk, chunk)]
        waiter(rows, block_send.at[0], block_recv.at[flow + part]).wait_recv()

    def arrived(flow, at_line, at_row):
        waiter(
            blocks_ref.at[at_line, at_row], block_send.at[0], block_recv.at[flow]
        ).wait_recv()

    def detour_out(part):
        rows = pl.ds(part * chunk, chunk)
        pltpu.make_async_remote_copy(
            src_ref=blocks_ref.at[line, row, rows],
            dst_ref=detour_ref.at[rows],
            send_sem=block_send.at[0],
            recv_sem=detour_recv.at[part],
            device_id=other_plane(row),
            device_id_type=pl.DeviceIdType.MESH,
        ).start()

    def detour_on(part):
        rows = pl.ds(part * chunk, chunk)
        waiter(detour_ref.at[rows], block_send.at[0], detour_recv.at[part]).wait_recv()
        pltpu.make_async_remote_copy(
            src_ref=detour_ref.at[rows],
            dst_ref=blocks_ref.at[line, hub - 1, rows],
            send_sem=block_send.at[2],
            recv_sem=block_recv.at[NEAR + part],
            device_id=other_plane(hub - 1),
            device_id_type=pl.DeviceIdType.MESH,
        ).start()

    def tell_ids(where):
        pltpu.make_async_remote_copy(
            src_ref=ids_ref.at[me],
            dst_ref=ids_ref.at[me],
            send_sem=ids_send,
            recv_sem=ids_recv,
            device_id=where,
            device_id_type=pl.DeviceIdType.MESH,
        ).start()

    def told_ids(count):
        waiter(ids_ref.at[pl.ds(0, count)], ids_send, ids_recv).wait_send()

    def hear_ids(count):
        waiter(ids_ref.at[pl.ds(0, count)], ids_send, ids_recv).wait_recv()

    def give(at_row, at_col, at_core, best):
        at = spot(at_col * CORES + at_core, at_row)
        given_ref[at] = best
        pltpu.make_async_remote_copy(
            src_ref=given_ref.at[at],
            dst_ref=taken_ref.at[me],
            send_sem=best_send,
            recv_sem=best_recv,
            device_id=device(at_row, at_col, at_core),
            device_id_type=pl.DeviceIdType.MESH,
        ).start()

    def gave(count):
        waiter(given_ref.at[pl.ds(0, count)], best_send, best_recv).wait_send()

    def take(*places):
        with jax.named_scope("w_back"):
            waiter(given_ref.at[pl.ds(0, len(places))], best_send, best_recv).wait_recv()
        best = taken_ref[spot(places[0][0], places[0][1])]
        for at_line, at_row in places[1:]:
            best = jnp.maximum(best, taken_ref[spot(at_line, at_row)])
        return best

    def finish(best):
        out_ref[...] = jnp.where(best > SAME / 2, jnp.maximum(best - SAME, -1.0), -1.0)

    def mark(at_line, at_row):
        shape = (row_count, row_count)
        down = jnp.transpose(jnp.broadcast_to(ids_ref[spot(at_line, at_row)], shape))
        here = down == lax.broadcasted_iota(jnp.int32, shape, 1)
        marks_ref[at_line, at_row] = jnp.where(here, SAME**0.5, 0.0).astype(jnp.bfloat16)

    def flat(ref, *index):
        values = ref[index]
        return values.reshape(-1, values.shape[-1])

    def operand(*indices):
        return jnp.concatenate(
            [
                jnp.concatenate([flat(blocks_ref, *index), flat(marks_ref, *index)], axis=1)
                for index in indices
            ],
            axis=0,
        )

    def scores(left, right):
        return lax.dot_general(
            left, right, (((1,), (1,)), ((), ())), preferred_element_type=jnp.float32
        )

    def down_max(values):
        return jnp.max(values, axis=0, keepdims=True)

    def fold(values):
        folded = values[:, :row_count]
        for at in range(1, values.shape[1] // row_count):
            folded = jnp.maximum(folded, values[:, at * row_count : (at + 1) * row_count])
        return folded

    def turn_max(folded):
        return down_max(jnp.transpose(folded))

    def without_self(values, start):
        down = lax.broadcasted_iota(jnp.int32, values.shape, 0)
        return jnp.where(
            down == lax.broadcasted_iota(jnp.int32, values.shape, 1) + start, -1.0, values
        )

    chip = pl.ds(col * CORES, CORES)

    def split(values):
        low, high = values[:, :row_count], values[:, row_count:]
        return jnp.where(core == 0, low, high), jnp.where(core == 0, high, low)

    def own_best():
        return down_max(
            without_self(scores(operand((chip, row)), operand((line, row))), core * row_count)
        )

    for copy in small_copies:
        copy.wait()
    counts = jnp.transpose(
        jnp.broadcast_to(lengths_ref[...].astype(jnp.float32), (row_count, row_count))
    )[:, 0:1]
    states_copy.wait()
    states = states_ref[...]
    summed = states[:, 0, :].astype(jnp.float32)
    for position in range(1, seq_len):
        token = states[:, position, :].astype(jnp.float32)
        summed = summed + jnp.where(counts > position, token, 0.0)
    pooled = (summed / counts).astype(jnp.bfloat16)
    weight_copy.wait()
    hidden = jnp.tanh(
        jnp.dot(pooled, weight_ref[...], preferred_element_type=jnp.float32) + bias_ref[...]
    )
    factor = lax.rsqrt(jnp.sum(hidden * hidden, axis=1, keepdims=True) + 1e-06)
    blocks_ref[line, row] = (hidden * factor).astype(jnp.bfloat16)

    with jax.named_scope("w_barrier"):
        pl.semaphore_wait(barrier, greetings)

    each_to(tell_ids)

    @pl.when((row != hub) & jnp.logical_not(around))
    def _():
        flow = jnp.where(row == 0, END, jnp.where(row == 1, NEAR, OUTER))
        for part in range(CHUNKS):
            rows = blocks_ref.at[line, row, pl.ds(part * chunk, chunk)]
            pltpu.make_async_remote_copy(
                src_ref=rows,
                dst_ref=rows,
                send_sem=block_send.at[0],
                recv_sem=block_recv.at[flow + part],
                device_id=device(hub, col, core),
                device_id_type=pl.DeviceIdType.MESH,
            ).start()

    @pl.when((row != hub) & around)
    def _():
        for part in range(CHUNKS):
            detour_out(part)

    for part in range(CHUNKS):
        send(ACROSS, part, line, row, device(row, far_col, core))
    for part in range(CHUNKS):
        send(SIBLING, part, line, row, sibling_device)
    mark(line, row)

    @pl.when(row != hub)
    def _():
        for part in range(CHUNKS):
            arrive(ACROSS, part, across_line, row)

            @pl.when(row == 1)
            def _():
                send(AFTER, part, across_line, row, device(0, col, core), 1)

            @pl.when((row > hub) & (core == 0))
            def _():
                send(CORNER, part, across_line, row, device(hub, col, core), 1)

        arrived(SIBLING, sibling_line, row)

        @pl.when(row > 0)
        def _():
            hear_ids(2)

        @pl.when(row == 0)
        def _():
            hear_ids(3)

        mark(across_line, row)
        mark(sibling_line, row)
        both = operand((chip, row))
        mine, other = split(down_max(scores(operand((across_line, row)), both)))
        best_ref[0:1] = jnp.maximum(mine, own_best())
        best_ref[1:2] = other

        @pl.when(row == 0)
        def _():
            with jax.named_scope("w_after"):
                arrived(AFTER, across_line, 1)
            mark(across_line, 1)
            after = scores(operand((across_line, 1)), operand((chip, row)))
            give(1, far_col, core, turn_max(fold(after)))
            mine, other = split(down_max(after))
            best_ref[0:1] = jnp.maximum(best_ref[0:1], mine)
            best_ref[1:2] = jnp.maximum(best_ref[1:2], other)

        give(row, col, far_core, best_ref[1:2])
        sent(0, 3)
        hubs = tuple((col * CORES + at_core, hub) for at_core in range(CORES))

        @pl.when(row == 0)
        def _():
            told_ids(4)
            gave(2)
            finish(jnp.maximum(best_ref[0:1], take((sibling_line, row), *hubs)))

        @pl.when(row == 1)
        def _():
            told_ids(5)
            gave(1)
            sent(1, 1)
            finish(
                jnp.maximum(best_ref[0:1], take((sibling_line, row), (across_line, 0), *hubs))
            )

        @pl.when(row > hub)
        def _():
            told_ids(4)
            gave(1)

            @pl.when(core == 0)
            def _():
                sent(1, 1)

            finish(
                jnp.maximum(best_ref[0:1], take((sibling_line, row), (line, hub), (across_line, hub)))
            )

    @pl.when(row == hub)
    def _():
        outer, beside, corner = (line, hub + 1), (across_line, hub), (across_line, hub + 1)
        near, end = (line, hub - 1), (line, 0)
        near_too, end_too = [(sibling_line, at) for at in (hub - 1, 0)]
        width = CORES * row_count

        def detour(part):
            @pl.when(around)
            def _():
                detour_on(part)

        def pass_outer(part):
            arrive(OUTER, part, *outer)

            @pl.when(core == 1)
            def _():
                send(CORNER, part, *outer, device(hub, far_col, core), 2)

        def pass_near(part):
            arrive(NEAR, part, *near)
            send(NEAR_TOO, part, *near, sibling_device, 1)

        def pass_end(part):
            arrive(END, part, *end)
            send(END_TOO, part, *end, sibling_device, 1)

        def pick(values, at):
            low, high = [
                values[:, (2 * at_core + at) * row_count : (2 * at_core + at + 1) * row_count]
                for at_core in range(CORES)
            ]
            return jnp.where(core == 0, low, high), jnp.where(core == 0, high, low)

        with jax.named_scope("w_a"):
            for part in range(2):
                detour(part)
                pass_outer(part)
                pass_end(part)
        with jax.named_scope("w_ids"):
            hear_ids(8)
        for at_row in range(hub + 1):
            mark(sibling_line, at_row)
        for place in (outer, near, end, beside, corner):
            mark(*place)
        with jax.named_scope("w_b"):
            for part in range(2, CHUNKS):
                detour(part)
                pass_outer(part)
                pass_end(part)
        arrived(SIBLING, sibling_line, hub)
        with jax.named_scope("w_near1"):
            for part in range(2):
                pass_near(part)
        with jax.named_scope("w_beside"):
            for part in range(CHUNKS):
                arrive(ACROSS, part, *beside)
        with jax.named_scope("w_end_too"):
            arrived(END_TOO, *end_too)
        mine_first = operand((line, hub), outer, beside)
        early = scores(mine_first, operand((chip, hub), (chip, 0)))
        own = without_self(early[:row_count, : CORES * row_count], -core * row_count)
        early = jnp.concatenate(
            [jnp.concatenate([own, early[:row_count, CORES * row_count :]], axis=1), early[row_count:]],
            axis=0,
        )
        early_best = down_max(early)
        folded_ref[...] = fold(early)
        with jax.named_scope("w_near"):
            for part in range(2, CHUNKS):
                pass_near(part)
        with jax.named_scope("w_near_too"):
            arrived(NEAR_TOO, *near_too)
        near_scores = scores(operand((line, hub), outer, beside, end), operand((chip, hub - 1)))
        near_best = down_max(near_scores)
        folded = jnp.maximum(folded_ref[...], fold(near_scores[: 3 * row_count]))
        best_ref[0:1] = turn_max(folded[:row_count])
        give(hub + 1, col, core, turn_max(folded[row_count : 2 * row_count]))
        give(hub, far_col, core, turn_max(folded[2 * row_count :]))
        end_best = turn_max(fold(near_scores[3 * row_count :]))
        with jax.named_scope("w_corner"):
            arrived(CORNER, *corner)
        corner_scores = scores(operand(corner), operand((chip, hub), (chip, 0), (chip, hub - 1)))
        last = down_max(corner_scores)
        hub_mine, hub_other = split(jnp.maximum(early_best, last[:, : 2 * width])[:, :width])
        end_mine, end_other = split(jnp.maximum(early_best, last[:, : 2 * width])[:, width:])
        near_mine, near_other = split(jnp.maximum(near_best, last[:, 2 * width :]))
        give(0, col, core, jnp.maximum(end_best, end_mine))
        give(0, col, far_core, end_other)
        give(hub - 1, col, core, near_mine)
        give(hub - 1, col, far_core, near_other)
        give(hub, col, far_core, hub_other)
        give(hub + 1, far_col, core, turn_max(fold(corner_scores)))
        best_ref[0:1] = jnp.maximum(best_ref[0:1], hub_mine)
        sent(0, 2)
        sent(1, 2)

        @pl.when(core == 1)
        def _():
            sent(2, 2)

        told_ids(2)
        gave(8)
        finish(jnp.maximum(best_ref[0:1], take((sibling_line, hub), (across_line, hub))))


def meet_body(token_states, lengths, cluster_id, proj_weight, proj_bias):
    row_count, seq_len, feat_dim = token_states.shape
    lines = lax.axis_size("docs") // ROWS * CORES
    vmem = pl.BlockSpec(memory_space=pltpu.VMEM)
    hbm = pl.BlockSpec(memory_space=pl.ANY)
    result = pl.pallas_call(
        meet_kernel,
        out_shape=pltpu.VMEM((1, row_count), jnp.float32),
        in_specs=[hbm] * 5,
        out_specs=vmem,
        scratch_shapes=[
            pltpu.VMEM((1, row_count), jnp.int32),
            pltpu.VMEM((1, feat_dim), jnp.float32),
            pltpu.VMEM(token_states.shape, jnp.bfloat16),
            pltpu.VMEM(proj_weight.shape, jnp.bfloat16),
            pltpu.VMEM((lines * ROWS, 1, row_count), jnp.int32),
            pltpu.VMEM((lines, ROWS, row_count, feat_dim), jnp.bfloat16),
            pltpu.VMEM((lines, ROWS, row_count, row_count), jnp.bfloat16),
            pltpu.VMEM((row_count, feat_dim), jnp.bfloat16),
            pltpu.VMEM((2, row_count), jnp.float32),
            pltpu.VMEM((3 * row_count, row_count), jnp.float32),
            pltpu.VMEM((lines * ROWS, 1, row_count), jnp.float32),
            pltpu.VMEM((lines * ROWS, 1, row_count), jnp.float32),
            pltpu.SemaphoreType.DMA((3,)),
            pltpu.SemaphoreType.DMA,
            pltpu.SemaphoreType.DMA,
            pltpu.SemaphoreType.DMA((3,)),
            pltpu.SemaphoreType.DMA((FLOWS,)),
            pltpu.SemaphoreType.DMA((CHUNKS,)),
            pltpu.SemaphoreType.DMA,
            pltpu.SemaphoreType.DMA,
            pltpu.SemaphoreType.DMA,
            pltpu.SemaphoreType.DMA,
        ],
        compiler_params=pltpu.CompilerParams(collective_id=0, has_side_effects=True),
        name="scores",
    )(token_states, lengths[None, :], cluster_id[None, :], proj_weight, proj_bias[None, :])
    return result.reshape(row_count)

def solution(mesh):
    in_specs = (
        P(("groups", "docs", "help"), None, None),
        P(("groups", "docs", "help")),
        P(("groups", "docs", "help")),
        P(),
        P(),
    )
    out_specs = P(("groups", "docs", "help"))
    meets = mesh.shape["docs"] == 2 * ROWS and mesh.shape["help"] == CORES and mesh.shape["groups"] == 2
    return jax.shard_map(meet_body if meets else body, mesh=mesh, in_specs=in_specs, out_specs=out_specs, check_vma=False)
```

time: 24 us -> 21.9 us (0.912)
  Pallas kernels: 23.3 us -> 21.1 us
    pallas_call x1, Pallas kernels: 23.3 us -> 21.1 us  [meet_body(): pl.pallas_call(meet_kernel, out_shape=pltpu.VMEM((1, row_count), jnp.floa...]
where the time goes in v1:
time: 21.9 us; the launch traced here: 21.6 us
  Pallas kernels  21.1 us (96%)
  local copies, waits for them, and re-layouts  0.51 us (2%)
    pallas_call x1, Pallas kernels, meet_body(): pl.pallas_call(meet_kernel, out_shape=pltpu.VMEM((1, row_count), jnp.floa...  21.1 us
    unnamed x1, local copies, waits for them, and re-layouts  0.51 us

profile of v1, /device:TPU:0, one launch (start us, length us, event | category | flops | bytes accessed | tf_op | source)
XLA Modules:
  0.0 21.6 jit_solution(7484418807935133955)
XLA Ops:
  0.0 21.1 %scores.1 = f32[1,128]{1,0:T(1,128)S(1)} custom-call(bf16[128,2,1024]{2,1,0:T(2,128)(2,1)} %states_hbm.1, s32[1,128]{1,0:T(1,128)} %bitcast.6, s32[1,128]{1,0:T(1,128)} %bitcast.7, bf16[1024,1024]{1,0:T(8,128)(2,1)} %weight_hbm.1, f32[1,1024]{1,0:T(1,128)} %bitcast.5), custom_call_target="tpu_custom_call" | custom-call | tf_op jit(solution)/shard_map/scores/pallas_call | solution.py:612
  21.1 0.5 %copy.7 = f32[128]{0:T(128)} copy(f32[128]{0:T(128)S(1)} %bitcast.4) | data formatting | bytes 1024

commit v2 on v1

--- a/solution.py
+++ b/solution.py
@@ -82,8 +82,11 @@
 ROWS = 4
 CORES = 2
 CHUNKS = 4
+SLABS = 2
+KEPT = 4
+ROUND = 1
 SAME = 4.0
-SIBLING, CORNER, NEAR_TOO, END_TOO, AFTER = range(5)
+SIBLING, CORNER, NEAR_TOO, END_TOO, OUTER_TOO, BESIDE_TOO, AFTER = range(7)
 ACROSS, OUTER, NEAR, END = (AFTER + 1 + CHUNKS * at for at in range(4))
 FLOWS = END + CHUNKS
 
@@ -159,8 +162,17 @@
         copy.start()
     states_copy = pltpu.make_async_copy(states_hbm, states_ref, states_sem)
     states_copy.start()
-    weight_copy = pltpu.make_async_copy(weight_hbm, weight_ref, weight_sem)
-    weight_copy.start()
+    slab = feat_dim // SLABS
+    weight_copies = [
+        pltpu.make_async_copy(
+            weight_hbm.at[pl.ds(at * slab, slab)],
+            weight_ref.at[pl.ds(at * slab, slab)],
+            weight_sem.at[at],
+        )
+        for at in range(SLABS)
+    ]
+    for copy in weight_copies:
+        copy.start()
 
     barrier = pltpu.get_barrier_semaphore()
 
@@ -170,10 +182,11 @@
                 barrier, inc=1, device_id=where, device_id_type=pl.DeviceIdType.MESH
             )
 
-    around = (core == 1) & ((row == 1) | (row == hub))
+    around = (core == 1) | (group == 1)
+    passing = (core == 1) | (group == 0)
 
     def each_to(act):
-        @pl.when(row < hub)
+        @pl.when(row != hub)
         def _():
             for at_core in range(CORES):
                 act(device(hub, col, at_core))
@@ -182,9 +195,12 @@
         def _():
             act(device(0, far_col, core))
 
+        @pl.when(row == hub)
+        def _():
+            act(device(hub, far_col, far_core))
+
         @pl.when(row > hub)
         def _():
-            act(device(hub, col, core))
             act(device(hub, far_col, core))
 
         act(device(row, far_col, core))
@@ -202,25 +218,30 @@
 
     @pl.when(row == hub)
     def _():
-        for at_row in range(hub):
+        for at_row in (0, 1, hub + 1):
             for at_core in range(CORES):
                 greet(device(at_row, col, at_core))
-        greet(device(hub + 1, col, core), device(hub + 1, far_col, core))
-
-    @pl.when(around)
+        greet(device(hub + 1, far_col, core))
+
+    @pl.when((row == 1) & around)
     def _():
         greet(other_plane(row))
 
-        @pl.when(row == hub)
-        def _():
-            greet(other_plane(hub - 1))
+    @pl.when((row == hub) & passing)
+    def _():
+        greet(other_plane(row), other_plane(hub - 1))
+
+    @pl.when((row == hub) & around & jnp.logical_not((core == 1) & passing))
+    def _():
+        greet(other_plane(hub - 1))
 
     greetings = (
         2
         + 4 * (row < hub)
-        + 6 * (row == hub)
-        + 2 * (row > hub)
-        + around * (1 + (row == hub))
+        + 8 * (row == hub)
+        + 3 * (row > hub)
+        + ((row == 1) & around)
+        + (row == hub) * (1 + passing)
     )
 
     def send(flow, part, at_line, at_row, where, lane=0):
@@ -249,6 +270,10 @@
             blocks_ref.at[0, pl.ds(0, count)], block_send.at[lane], block_recv.at[0]
         ).wait_send()
 
+    def sent_parts(lane, count):
+        rows = blocks_ref.at[0, 0, pl.ds(0, count * chunk)]
+        waiter(rows, block_send.at[lane], block_recv.at[0]).wait_send()
+
     def arrive(flow, part, at_line, at_row):
         rows = blocks_ref.at[at_line, at_row, pl.ds(part * chunk, chunk)]
         waiter(rows, block_send.at[0], block_recv.at[flow + part]).wait_recv()
@@ -275,7 +300,7 @@
         pltpu.make_async_remote_copy(
             src_ref=detour_ref.at[rows],
             dst_ref=blocks_ref.at[line, hub - 1, rows],
-            send_sem=block_send.at[2],
+            send_sem=block_send.at[3],
             recv_sem=block_recv.at[NEAR + part],
             device_id=other_plane(hub - 1),
             device_id_type=pl.DeviceIdType.MESH,
@@ -388,10 +413,14 @@
         token = states[:, position, :].astype(jnp.float32)
         summed = summed + jnp.where(counts > position, token, 0.0)
     pooled = (summed / counts).astype(jnp.bfloat16)
-    weight_copy.wait()
-    hidden = jnp.tanh(
-        jnp.dot(pooled, weight_ref[...], preferred_element_type=jnp.float32) + bias_ref[...]
-    )
+    projected = bias_ref[...]
+    for at, copy in enumerate(weight_copies):
+        copy.wait()
+        depth_at = slice(at * slab, (at + 1) * slab)
+        projected = projected + jnp.dot(
+            pooled[:, depth_at], weight_ref[depth_at], preferred_element_type=jnp.float32
+        )
+    hidden = jnp.tanh(projected)
     factor = lax.rsqrt(jnp.sum(hidden * hidden, axis=1, keepdims=True) + 1e-06)
     blocks_ref[line, row] = (hidden * factor).astype(jnp.bfloat16)
 
@@ -400,10 +429,15 @@
 
     each_to(tell_ids)
 
-    @pl.when((row != hub) & jnp.logical_not(around))
-    def _():
-        flow = jnp.where(row == 0, END, jnp.where(row == 1, NEAR, OUTER))
-        for part in range(CHUNKS):
+    flow = jnp.where(row == 0, END, jnp.where(row == 1, NEAR, OUTER))
+    for part in range(CHUNKS):
+        if part < CHUNKS - ROUND:
+            detours = (row == 1) & (core == 1)
+        else:
+            detours = (row == 1) & around
+
+        @pl.when((row != hub) & jnp.logical_not(detours))
+        def _():
             rows = blocks_ref.at[line, row, pl.ds(part * chunk, chunk)]
             pltpu.make_async_remote_copy(
                 src_ref=rows,
@@ -414,16 +448,29 @@
                 device_id_type=pl.DeviceIdType.MESH,
             ).start()
 
-    @pl.when((row != hub) & around)
-    def _():
+        @pl.when(detours)
+        def _():
+            detour_out(part)
+
+    for part in range(CHUNKS):
+        send(SIBLING, part, line, row, sibling_device, 4)
+
+    def send_across():
         for part in range(CHUNKS):
-            detour_out(part)
-
-    for part in range(CHUNKS):
-        send(ACROSS, part, line, row, device(row, far_col, core))
-    for part in range(CHUNKS):
-        send(SIBLING, part, line, row, sibling_device)
+            send(ACROSS, part, line, row, device(row, far_col, core), 4)
+
+    later = (row > hub) & (core == 1)
+
+    @pl.when(jnp.logical_not(later))
+    def _():
+        send_across()
+
     mark(line, row)
+
+    @pl.when(later)
+    def _():
+        sent(0, 1)
+        send_across()
 
     @pl.when(row != hub)
     def _():
@@ -434,9 +481,11 @@
             def _():
                 send(AFTER, part, across_line, row, device(0, col, core), 1)
 
-            @pl.when((row > hub) & (core == 0))
-            def _():
-                send(CORNER, part, across_line, row, device(hub, col, core), 1)
+            if part < KEPT:
+
+                @pl.when((row > hub) & (core == 0))
+                def _():
+                    send(CORNER, part, across_line, row, device(hub, col, core), 1)
 
         arrived(SIBLING, sibling_line, row)
 
@@ -467,7 +516,12 @@
             best_ref[1:2] = jnp.maximum(best_ref[1:2], other)
 
         give(row, col, far_core, best_ref[1:2])
-        sent(0, 3)
+        sent(4, 2)
+
+        @pl.when(jnp.logical_not(later))
+        def _():
+            sent(0, 1)
+
         hubs = tuple((col * CORES + at_core, hub) for at_core in range(CORES))
 
         @pl.when(row == 0)
@@ -487,33 +541,38 @@
 
         @pl.when(row > hub)
         def _():
-            told_ids(4)
+            told_ids(5)
             gave(1)
 
             @pl.when(core == 0)
             def _():
-                sent(1, 1)
+                sent_parts(1, KEPT)
 
             finish(
-                jnp.maximum(best_ref[0:1], take((sibling_line, row), (line, hub), (across_line, hub)))
+                jnp.maximum(best_ref[0:1], take((sibling_line, row), (across_line, hub), *hubs))
             )
 
     @pl.when(row == hub)
     def _():
         outer, beside, corner = (line, hub + 1), (across_line, hub), (across_line, hub + 1)
         near, end = (line, hub - 1), (line, 0)
-        near_too, end_too = [(sibling_line, at) for at in (hub - 1, 0)]
+        near_too, end_too, outer_too = [(sibling_line, at) for at in (hub - 1, 0, hub + 1)]
+        beside_too = (far_col * CORES + far_core, hub)
+        far_chip = pl.ds(far_col * CORES, CORES)
         width = CORES * row_count
 
         def detour(part):
-            @pl.when(around)
+            passes = passing if part >= CHUNKS - ROUND else core == 1
+
+            @pl.when(passes)
             def _():
                 detour_on(part)
 
         def pass_outer(part):
             arrive(OUTER, part, *outer)
-
-            @pl.when(core == 1)
+            send(OUTER_TOO, part, *outer, sibling_device, 1)
+
+            @pl.when(True if part >= KEPT else core == 1)
             def _():
                 send(CORNER, part, *outer, device(hub, far_col, core), 2)
 
@@ -538,10 +597,10 @@
                 pass_outer(part)
                 pass_end(part)
         with jax.named_scope("w_ids"):
-            hear_ids(8)
-        for at_row in range(hub + 1):
+            hear_ids(10)
+        for at_row in range(ROWS):
             mark(sibling_line, at_row)
-        for place in (outer, near, end, beside, corner):
+        for place in (outer, near, end, beside, beside_too, corner):
             mark(*place)
         with jax.named_scope("w_b"):
             for part in range(2, CHUNKS):
@@ -549,59 +608,79 @@
                 pass_outer(part)
                 pass_end(part)
         arrived(SIBLING, sibling_line, hub)
-        with jax.named_scope("w_near1"):
-            for part in range(2):
-                pass_near(part)
         with jax.named_scope("w_beside"):
             for part in range(CHUNKS):
                 arrive(ACROSS, part, *beside)
-        with jax.named_scope("w_end_too"):
+                send(BESIDE_TOO, part, *beside, sibling_device, 1)
+        with jax.named_scope("w_near1"):
+            pass_near(0)
+        early = scores(operand((line, hub), outer, beside, end), operand((chip, hub)))
+        own = without_self(early[:row_count], -core * row_count)
+        hub_best = jnp.maximum(down_max(own), down_max(early[row_count:]))
+        folded_ref[...] = fold(early[row_count:])
+        with jax.named_scope("w_near"):
+            for part in range(1, CHUNKS):
+                pass_near(part)
+        with jax.named_scope("w_too"):
+            arrived(OUTER_TOO, *outer_too)
+            arrived(BESIDE_TOO, *beside_too)
             arrived(END_TOO, *end_too)
-        mine_first = operand((line, hub), outer, beside)
-        early = scores(mine_first, operand((chip, hub), (chip, 0)))
-        own = without_self(early[:row_count, : CORES * row_count], -core * row_count)
-        early = jnp.concatenate(
-            [jnp.concatenate([own, early[:row_count, CORES * row_count :]], axis=1), early[row_count:]],
-            axis=0,
-        )
-        early_best = down_max(early)
-        folded_ref[...] = fold(early)
-        with jax.named_scope("w_near"):
-            for part in range(2, CHUNKS):
-                pass_near(part)
+        right_scores = scores(operand(end, near, beside), operand((chip, hub + 1), (far_chip, hub)))
+        end_scores = scores(operand(near), operand((chip, 0)))
+        left_size = 2 * row_count
+        mine, other = split(down_max(right_scores[:, :width]))
+        give(hub + 1, col, far_core, other)
+        give(hub + 1, col, core, jnp.maximum(turn_max(folded_ref[:row_count]), mine))
+        end_folded = jnp.maximum(folded_ref[2 * row_count :], fold(right_scores[:row_count]))
+        near_folded = jnp.maximum(fold(end_scores), fold(right_scores[row_count:left_size]))
+        end_best = down_max(end_scores)
+        end_turned = turn_max(end_folded)
+        beside_folded = jnp.maximum(
+            folded_ref[row_count:left_size], fold(right_scores[left_size:, :width])
+        )
+        beside_best = down_max(right_scores[:left_size, width:])
         with jax.named_scope("w_near_too"):
             arrived(NEAR_TOO, *near_too)
-        near_scores = scores(operand((line, hub), outer, beside, end), operand((chip, hub - 1)))
-        near_best = down_max(near_scores)
-        folded = jnp.maximum(folded_ref[...], fold(near_scores[: 3 * row_count]))
-        best_ref[0:1] = turn_max(folded[:row_count])
-        give(hub + 1, col, core, turn_max(folded[row_count : 2 * row_count]))
-        give(hub, far_col, core, turn_max(folded[2 * row_count :]))
-        end_best = turn_max(fold(near_scores[3 * row_count :]))
         with jax.named_scope("w_corner"):
             arrived(CORNER, *corner)
-        corner_scores = scores(operand(corner), operand((chip, hub), (chip, 0), (chip, hub - 1)))
+        corner_scores = scores(operand(corner), operand((chip, 0), (chip, hub - 1)))
         last = down_max(corner_scores)
-        hub_mine, hub_other = split(jnp.maximum(early_best, last[:, : 2 * width])[:, :width])
-        end_mine, end_other = split(jnp.maximum(early_best, last[:, : 2 * width])[:, width:])
-        near_mine, near_other = split(jnp.maximum(near_best, last[:, 2 * width :]))
-        give(0, col, core, jnp.maximum(end_best, end_mine))
-        give(0, col, far_core, end_other)
-        give(hub - 1, col, core, near_mine)
+        mine, other = split(jnp.maximum(end_best, last[:, :width]))
+        give(0, col, core, jnp.maximum(end_turned, mine))
+        give(0, col, far_core, other)
+        give(hub + 1, far_col, core, turn_max(fold(corner_scores)))
+        hub_scores = scores(operand(near), operand((chip, hub)))
+        near_mine, near_other = split(last[:, width:])
         give(hub - 1, col, far_core, near_other)
+        near_turned = turn_max(jnp.maximum(near_folded, fold(hub_scores)))
+        give(hub - 1, col, core, jnp.maximum(near_turned, near_mine))
+        mine, other = split(beside_best)
+        give(hub, far_col, core, jnp.maximum(turn_max(beside_folded), mine))
+        give(hub, far_col, far_core, other)
+        hub_mine, hub_other = split(jnp.maximum(hub_best, down_max(hub_scores)))
         give(hub, col, far_core, hub_other)
-        give(hub + 1, far_col, core, turn_max(fold(corner_scores)))
-        best_ref[0:1] = jnp.maximum(best_ref[0:1], hub_mine)
-        sent(0, 2)
-        sent(1, 2)
+        best_ref[0:1] = hub_mine
+        with jax.named_scope("w_sent"):
+            pass
+        sent(4, 2)
+        sent(1, 4)
 
         @pl.when(core == 1)
         def _():
-            sent(2, 2)
-
-        told_ids(2)
-        gave(8)
-        finish(jnp.maximum(best_ref[0:1], take((sibling_line, hub), (across_line, hub))))
+            sent(2, 1)
+            sent(3, 1)
+
+        @pl.when(core == 0)
+        def _():
+            pass
+
+        @pl.when((core == 0) & passing)
+        def _():
+            sent_parts(3, ROUND)
+
+        told_ids(3)
+        gave(10)
+        finish(jnp.maximum(best_ref[0:1], take((sibling_line, hub), (across_line, hub), beside_too)))
 
 
 def meet_body(token_states, lengths, cluster_id, proj_weight, proj_bias):
@@ -629,8 +708,8 @@
             pltpu.VMEM((lines * ROWS, 1, row_count), jnp.float32),
             pltpu.SemaphoreType.DMA((3,)),
             pltpu.SemaphoreType.DMA,
-            pltpu.SemaphoreType.DMA,
-            pltpu.SemaphoreType.DMA((3,)),
+            pltpu.SemaphoreType.DMA((SLABS,)),
+            pltpu.SemaphoreType.DMA((5,)),
             pltpu.SemaphoreType.DMA((FLOWS,)),
             pltpu.SemaphoreType.DMA((CHUNKS,)),
             pltpu.SemaphoreType.DMA,

time: 21.9 us -> 20.8 us (0.950)
  Pallas kernels: 21.1 us -> 20.1 us
    pallas_call x1, Pallas kernels: 21.1 us -> 20.1 us  [meet_body(): pl.pallas_call(meet_kernel, out_shape=pltpu.VMEM((1, row_count), jnp.floa...]
where the time goes in v2:
time: 20.8 us; the launch traced here: 20.6 us
  Pallas kernels  20.1 us (97%)
  local copies, waits for them, and re-layouts  0.51 us (2%)
    pallas_call x1, Pallas kernels, meet_body(): pl.pallas_call(meet_kernel, out_shape=pltpu.VMEM((1, row_count), jnp.floa...  20.1 us
    unnamed x1, local copies, waits for them, and re-layouts  0.51 us

profile of v2, /device:TPU:0, one launch (start us, length us, event | category | flops | bytes accessed | tf_op | source)
XLA Modules:
  0.0 20.6 jit_solution(9664597599773282611)
XLA Ops:
  0.0 20.1 %scores.1 = f32[1,128]{1,0:T(1,128)S(1)} custom-call(bf16[128,2,1024]{2,1,0:T(2,128)(2,1)} %states_hbm.1, s32[1,128]{1,0:T(1,128)} %bitcast.6, s32[1,128]{1,0:T(1,128)} %bitcast.7, bf16[1024,1024]{1,0:T(8,128)(2,1)} %weight_hbm.1, f32[1,1024]{1,0:T(1,128)} %bitcast.5), custom_call_target="tpu_custom_call" | custom-call | tf_op jit(solution)/shard_map/scores/pallas_call | solution.py:691
  20.1 0.5 %copy.7 = f32[128]{0:T(128)} copy(f32[128]{0:T(128)S(1)} %bitcast.4) | data formatting | bytes 1024

commit v3 on v2

--- a/solution.py
+++ b/solution.py
@@ -152,6 +152,8 @@
     me = spot(line, row)
     sibling_device = device(row, col, far_core)
 
+    states_copy = pltpu.make_async_copy(states_hbm, states_ref, states_sem)
+    states_copy.start()
     small_copies = [
         pltpu.make_async_copy(source, held, small_sem.at[position])
         for position, (source, held) in enumerate(
@@ -160,8 +162,6 @@
     ]
     for copy in small_copies:
         copy.start()
-    states_copy = pltpu.make_async_copy(states_hbm, states_ref, states_sem)
-    states_copy.start()
     slab = feat_dim // SLABS
     weight_copies = [
         pltpu.make_async_copy(
@@ -171,8 +171,6 @@
         )
         for at in range(SLABS)
     ]
-    for copy in weight_copies:
-        copy.start()
 
     barrier = pltpu.get_barrier_semaphore()
 
@@ -234,6 +232,9 @@
     @pl.when((row == hub) & around & jnp.logical_not((core == 1) & passing))
     def _():
         greet(other_plane(hub - 1))
+
+    for copy in weight_copies:
+        copy.start()
 
     greetings = (
         2
@@ -401,12 +402,14 @@
             without_self(scores(operand((chip, row)), operand((line, row))), core * row_count)
         )
 
-    for copy in small_copies:
-        copy.wait()
+    with jax.named_scope('e_small'):
+        for copy in small_copies:
+            copy.wait()
     counts = jnp.transpose(
         jnp.broadcast_to(lengths_ref[...].astype(jnp.float32), (row_count, row_count))
     )[:, 0:1]
-    states_copy.wait()
+    with jax.named_scope('e_states'):
+        states_copy.wait()
     states = states_ref[...]
     summed = states[:, 0, :].astype(jnp.float32)
     for position in range(1, seq_len):
@@ -415,7 +418,8 @@
     pooled = (summed / counts).astype(jnp.bfloat16)
     projected = bias_ref[...]
     for at, copy in enumerate(weight_copies):
-        copy.wait()
+        with jax.named_scope('e_weight%d' % at):
+            copy.wait()
         depth_at = slice(at * slab, (at + 1) * slab)
         projected = projected + jnp.dot(
             pooled[:, depth_at], weight_ref[depth_at], preferred_element_type=jnp.float32
@@ -612,51 +616,58 @@
             for part in range(CHUNKS):
                 arrive(ACROSS, part, *beside)
                 send(BESIDE_TOO, part, *beside, sibling_device, 1)
-        with jax.named_scope("w_near1"):
-            pass_near(0)
-        early = scores(operand((line, hub), outer, beside, end), operand((chip, hub)))
+        left_size = 2 * row_count
+        hubs = operand((chip, hub))
+        early = scores(operand((line, hub), outer), hubs)
+        early_too = scores(operand(beside, end), hubs)
         own = without_self(early[:row_count], -core * row_count)
-        hub_best = jnp.maximum(down_max(own), down_max(early[row_count:]))
-        folded_ref[...] = fold(early[row_count:])
+        hub_best = jnp.maximum(
+            jnp.maximum(down_max(own), down_max(early[row_count:])), down_max(early_too)
+        )
+        early_folded = jnp.concatenate([fold(early[row_count:]), fold(early_too)], axis=0)
+        outer_early, beside_early, end_early = [
+            turn_max(early_folded[at * row_count : (at + 1) * row_count]) for at in range(3)
+        ]
         with jax.named_scope("w_near"):
-            for part in range(1, CHUNKS):
+            for part in range(CHUNKS):
                 pass_near(part)
         with jax.named_scope("w_too"):
             arrived(OUTER_TOO, *outer_too)
             arrived(BESIDE_TOO, *beside_too)
             arrived(END_TOO, *end_too)
-        right_scores = scores(operand(end, near, beside), operand((chip, hub + 1), (far_chip, hub)))
+        outer_scores = scores(operand(end, near, beside), operand((chip, hub + 1)))
+        beside_scores = scores(operand(end, near), operand((far_chip, hub)))
         end_scores = scores(operand(near), operand((chip, 0)))
-        left_size = 2 * row_count
-        mine, other = split(down_max(right_scores[:, :width]))
+        mine, other = split(down_max(outer_scores))
         give(hub + 1, col, far_core, other)
-        give(hub + 1, col, core, jnp.maximum(turn_max(folded_ref[:row_count]), mine))
-        end_folded = jnp.maximum(folded_ref[2 * row_count :], fold(right_scores[:row_count]))
-        near_folded = jnp.maximum(fold(end_scores), fold(right_scores[row_count:left_size]))
-        end_best = down_max(end_scores)
-        end_turned = turn_max(end_folded)
-        beside_folded = jnp.maximum(
-            folded_ref[row_count:left_size], fold(right_scores[left_size:, :width])
-        )
-        beside_best = down_max(right_scores[:left_size, width:])
+        give(hub + 1, col, core, jnp.maximum(outer_early, mine))
+        folded_ref[:left_size] = jnp.maximum(fold(outer_scores[:left_size]), fold(beside_scores))
+        folded_ref[row_count:left_size] = jnp.maximum(
+            folded_ref[row_count:left_size], fold(end_scores)
+        )
+        folded_ref[left_size:] = fold(outer_scores[left_size:])
+        end_low = down_max(end_scores)
+        beside_best = down_max(beside_scores)
+        with jax.named_scope("w_corner"):
+            arrived(CORNER, *corner)
+        corner_end = scores(operand(corner), operand((chip, 0)))
+        mine, other = split(jnp.maximum(end_low, down_max(corner_end)))
+        give(0, col, far_core, other)
+        end_best = jnp.maximum(end_early, turn_max(folded_ref[:row_count]))
+        give(0, col, core, jnp.maximum(end_best, mine))
         with jax.named_scope("w_near_too"):
             arrived(NEAR_TOO, *near_too)
-        with jax.named_scope("w_corner"):
-            arrived(CORNER, *corner)
-        corner_scores = scores(operand(corner), operand((chip, 0), (chip, hub - 1)))
-        last = down_max(corner_scores)
-        mine, other = split(jnp.maximum(end_best, last[:, :width]))
-        give(0, col, core, jnp.maximum(end_turned, mine))
-        give(0, col, far_core, other)
-        give(hub + 1, far_col, core, turn_max(fold(corner_scores)))
+        corner_near = scores(operand(corner), operand((chip, hub - 1)))
+        give(hub + 1, far_col, core, turn_max(jnp.maximum(fold(corner_end), fold(corner_near))))
+        near_mine, near_other = split(down_max(corner_near))
+        give(hub - 1, col, far_core, near_other)
         hub_scores = scores(operand(near), operand((chip, hub)))
-        near_mine, near_other = split(last[:, width:])
-        give(hub - 1, col, far_core, near_other)
-        near_turned = turn_max(jnp.maximum(near_folded, fold(hub_scores)))
-        give(hub - 1, col, core, jnp.maximum(near_turned, near_mine))
+        near_best = turn_max(jnp.maximum(folded_ref[row_count:left_size], fold(hub_scores)))
+        give(hub - 1, col, core, jnp.maximum(near_best, near_mine))
         mine, other = split(beside_best)
-        give(hub, far_col, core, jnp.maximum(turn_max(beside_folded), mine))
         give(hub, far_col, far_core, other)
+        beside_turned = jnp.maximum(beside_early, turn_max(folded_ref[left_size:]))
+        give(hub, far_col, core, jnp.maximum(beside_turned, mine))
         hub_mine, hub_other = split(jnp.maximum(hub_best, down_max(hub_scores)))
         give(hub, col, far_core, hub_other)
         best_ref[0:1] = hub_mine

time: 20.8 us -> 20.3 us (0.976)
  Pallas kernels: 20.1 us -> 19.7 us
    pallas_call x1, Pallas kernels: 20.1 us -> 19.7 us  [meet_body(): pl.pallas_call(meet_kernel, out_shape=pltpu.VMEM((1, row_count), jnp.floa...]
where the time goes in v3:
time: 20.3 us; the launch traced here: 20.2 us
  Pallas kernels  19.7 us (97%)
  local copies, waits for them, and re-layouts  0.51 us (3%)
    pallas_call x1, Pallas kernels, meet_body(): pl.pallas_call(meet_kernel, out_shape=pltpu.VMEM((1, row_count), jnp.floa...  19.7 us
    unnamed x1, local copies, waits for them, and re-layouts  0.51 us

profile of v3, /device:TPU:0, one launch (start us, length us, event | category | flops | bytes accessed | tf_op | source)
XLA Modules:
  0.0 20.2 jit_solution(10911519329652638804)
XLA Ops:
  0.0 19.7 %scores.1 = f32[1,128]{1,0:T(1,128)S(1)} custom-call(bf16[128,2,1024]{2,1,0:T(2,128)(2,1)} %states_hbm.1, s32[1,128]{1,0:T(1,128)} %bitcast.6, s32[1,128]{1,0:T(1,128)} %bitcast.7, bf16[1024,1024]{1,0:T(8,128)(2,1)} %weight_hbm.1, f32[1,1024]{1,0:T(1,128)} %bitcast.5), custom_call_target="tpu_custom_call" | custom-call | tf_op jit(solution)/shard_map/scores/pallas_call | solution.py:702
  19.7 0.5 %copy.7 = f32[128]{0:T(128)} copy(f32[128]{0:T(128)S(1)} %bitcast.4) | data formatting | bytes 1024

commit v4 on v3

--- a/solution.py
+++ b/solution.py
@@ -86,7 +86,7 @@
 KEPT = 4
 ROUND = 1
 SAME = 4.0
-SIBLING, CORNER, NEAR_TOO, END_TOO, OUTER_TOO, BESIDE_TOO, AFTER = range(7)
+SIBLING, CORNER, NEAR_TOO, END_TOO, OUTER_TOO, BESIDE_TOO, CORNER_TOO, AFTER = range(8)
 ACROSS, OUTER, NEAR, END = (AFTER + 1 + CHUNKS * at for at in range(4))
 FLOWS = END + CHUNKS
 
@@ -199,7 +199,8 @@
 
         @pl.when(row > hub)
         def _():
-            act(device(hub, far_col, core))
+            for at_core in range(CORES):
+                act(device(hub, far_col, at_core))
 
         act(device(row, far_col, core))
         act(sibling_device)
@@ -216,10 +217,10 @@
 
     @pl.when(row == hub)
     def _():
-        for at_row in (0, 1, hub + 1):
-            for at_core in range(CORES):
+        for at_core in range(CORES):
+            for at_row in (0, 1, hub + 1):
                 greet(device(at_row, col, at_core))
-        greet(device(hub + 1, far_col, core))
+            greet(device(hub + 1, far_col, at_core))
 
     @pl.when((row == 1) & around)
     def _():
@@ -239,8 +240,8 @@
     greetings = (
         2
         + 4 * (row < hub)
-        + 8 * (row == hub)
-        + 3 * (row > hub)
+        + 9 * (row == hub)
+        + 4 * (row > hub)
         + ((row == 1) & around)
         + (row == hub) * (1 + passing)
     )
@@ -539,22 +540,36 @@
             told_ids(5)
             gave(1)
             sent(1, 1)
-            finish(
-                jnp.maximum(best_ref[0:1], take((sibling_line, row), (across_line, 0), *hubs))
-            )
+
+            @pl.when(group == 0)
+            def _():
+                best = take((sibling_line, row), (across_line, 0), *hubs)
+                finish(jnp.maximum(best_ref[0:1], best))
+
+            @pl.when(group == 1)
+            def _():
+                best = take((sibling_line, row), (across_line, 0), (line, hub))
+                finish(jnp.maximum(best_ref[0:1], best))
 
         @pl.when(row > hub)
         def _():
-            told_ids(5)
+            told_ids(6)
             gave(1)
 
             @pl.when(core == 0)
             def _():
                 sent_parts(1, KEPT)
 
-            finish(
-                jnp.maximum(best_ref[0:1], take((sibling_line, row), (across_line, hub), *hubs))
-            )
+            @pl.when(group == 0)
+            def _():
+                best = take((sibling_line, row), (across_line, hub), *hubs)
+                finish(jnp.maximum(best_ref[0:1], best))
+
+            @pl.when(group == 1)
+            def _():
+                far_hub = (far_col * CORES + far_core, hub)
+                best = take((sibling_line, row), (across_line, hub), far_hub, *hubs)
+                finish(jnp.maximum(best_ref[0:1], best))
 
     @pl.when(row == hub)
     def _():
@@ -562,13 +577,13 @@
         near, end = (line, hub - 1), (line, 0)
         near_too, end_too, outer_too = [(sibling_line, at) for at in (hub - 1, 0, hub + 1)]
         beside_too = (far_col * CORES + far_core, hub)
+        corner_too = (far_col * CORES + far_core, hub + 1)
+        forward = group == 0
         far_chip = pl.ds(far_col * CORES, CORES)
         width = CORES * row_count
 
         def detour(part):
-            passes = passing if part >= CHUNKS - ROUND else core == 1
-
-            @pl.when(passes)
+            @pl.when(core == 1)
             def _():
                 detour_on(part)
 
@@ -582,7 +597,10 @@
 
         def pass_near(part):
             arrive(NEAR, part, *near)
-            send(NEAR_TOO, part, *near, sibling_device, 1)
+
+            @pl.when(forward)
+            def _():
+                send(NEAR_TOO, part, *near, sibling_device, 1)
 
         def pass_end(part):
             arrive(END, part, *end)
@@ -595,16 +613,21 @@
             ]
             return jnp.where(core == 0, low, high), jnp.where(core == 0, high, low)
 
+        @pl.when((core == 0) & passing)
+        def _():
+            for part in range(CHUNKS - ROUND, CHUNKS):
+                detour_on(part)
+
         with jax.named_scope("w_a"):
             for part in range(2):
                 detour(part)
                 pass_outer(part)
                 pass_end(part)
         with jax.named_scope("w_ids"):
-            hear_ids(10)
+            hear_ids(11)
         for at_row in range(ROWS):
             mark(sibling_line, at_row)
-        for place in (outer, near, end, beside, beside_too, corner):
+        for place in (outer, near, end, beside, beside_too, corner, corner_too):
             mark(*place)
         with jax.named_scope("w_b"):
             for part in range(2, CHUNKS):
@@ -624,55 +647,114 @@
         hub_best = jnp.maximum(
             jnp.maximum(down_max(own), down_max(early[row_count:])), down_max(early_too)
         )
-        early_folded = jnp.concatenate([fold(early[row_count:]), fold(early_too)], axis=0)
-        outer_early, beside_early, end_early = [
-            turn_max(early_folded[at * row_count : (at + 1) * row_count]) for at in range(3)
-        ]
-        with jax.named_scope("w_near"):
+        outer_early = turn_max(fold(early[row_count:]))
+        early_folded = fold(early_too)
+        outers, besides, ends = (chip, hub + 1), (far_chip, hub), (chip, 0)
+        with jax.named_scope("w_outer_too"):
+            arrived(OUTER_TOO, *outer_too)
+        beside_outer = scores(operand(beside), operand(outers))
+        end_outer = scores(operand(end), operand(outers))
+        outer_low = jnp.maximum(down_max(beside_outer), down_max(end_outer))
+        beside_early = turn_max(jnp.maximum(early_folded[:row_count], fold(beside_outer)))
+        end_early = turn_max(jnp.maximum(early_folded[row_count:], fold(end_outer)))
+
+        def give_outers(near_outer):
+            mine, other = split(jnp.maximum(outer_low, down_max(near_outer)))
+            give(hub + 1, col, far_core, other)
+            give(hub + 1, col, core, jnp.maximum(outer_early, mine))
+
+        def give_ends(best, folded):
+            mine, other = split(best)
+            give(0, col, far_core, other)
+            mine = jnp.maximum(jnp.maximum(end_early, mine), turn_max(folded))
+            give(0, col, core, mine)
+
+        def give_besides(best):
+            mine, other = split(best)
+            give(hub, far_col, far_core, other)
+            give(hub, far_col, core, jnp.maximum(beside_early, mine))
+
+        def give_hubs(hub_scores):
+            mine, other = split(jnp.maximum(hub_best, down_max(hub_scores)))
+            give(hub, col, far_core, other)
+            best_ref[0:1] = mine
+
+        @pl.when(group == 0)
+        def _():
+            with jax.named_scope("w_near"):
+                for part in range(CHUNKS):
+                    pass_near(part)
+            with jax.named_scope("w_too"):
+                arrived(BESIDE_TOO, *beside_too)
+                arrived(END_TOO, *end_too)
+            end_beside = scores(operand(end), operand(besides))
+            near_end = scores(operand(near), operand(ends))
+            with jax.named_scope("w_corner"):
+                arrived(CORNER, *corner)
+            corner_operand = operand(corner)
+            corner_end = jnp.concatenate(
+                [
+                    scores(corner_operand, operand((col * CORES + at_core, 0)))
+                    for at_core in range(CORES)
+                ],
+                axis=1,
+            )
+            give_ends(
+                jnp.maximum(down_max(near_end), down_max(corner_end)), fold(end_beside)
+            )
+            near_outer = scores(operand(near), operand(outers))
+            near_beside = scores(operand(near), operand(besides))
+            give_outers(near_outer)
+            near_folded = jnp.maximum(
+                fold(near_end), jnp.maximum(fold(near_outer), fold(near_beside))
+            )
+            with jax.named_scope("w_near_too"):
+                arrived(NEAR_TOO, *near_too)
+            corner_near = scores(operand(corner), operand((chip, hub - 1)))
+            hub_scores = scores(operand(near), hubs)
+            give(
+                hub + 1, far_col, core, turn_max(jnp.maximum(fold(corner_end), fold(corner_near)))
+            )
+            mine, other = split(down_max(corner_near))
+            give(hub - 1, col, far_core, other)
+            near_best = turn_max(jnp.maximum(near_folded, fold(hub_scores)))
+            give(hub - 1, col, core, jnp.maximum(near_best, mine))
+            give_besides(jnp.maximum(down_max(end_beside), down_max(near_beside)))
+            give_hubs(hub_scores)
+
+        @pl.when(group == 1)
+        def _():
+            with jax.named_scope("w_corner"):
+                arrived(CORNER, *corner)
             for part in range(CHUNKS):
-                pass_near(part)
-        with jax.named_scope("w_too"):
-            arrived(OUTER_TOO, *outer_too)
-            arrived(BESIDE_TOO, *beside_too)
-            arrived(END_TOO, *end_too)
-        outer_scores = scores(operand(end, near, beside), operand((chip, hub + 1)))
-        beside_scores = scores(operand(end, near), operand((far_chip, hub)))
-        end_scores = scores(operand(near), operand((chip, 0)))
-        mine, other = split(down_max(outer_scores))
-        give(hub + 1, col, far_core, other)
-        give(hub + 1, col, core, jnp.maximum(outer_early, mine))
-        folded_ref[:left_size] = jnp.maximum(fold(outer_scores[:left_size]), fold(beside_scores))
-        folded_ref[row_count:left_size] = jnp.maximum(
-            folded_ref[row_count:left_size], fold(end_scores)
-        )
-        folded_ref[left_size:] = fold(outer_scores[left_size:])
-        end_low = down_max(end_scores)
-        beside_best = down_max(beside_scores)
-        with jax.named_scope("w_corner"):
-            arrived(CORNER, *corner)
-        corner_end = scores(operand(corner), operand((chip, 0)))
-        mine, other = split(jnp.maximum(end_low, down_max(corner_end)))
-        give(0, col, far_core, other)
-        end_best = jnp.maximum(end_early, turn_max(folded_ref[:row_count]))
-        give(0, col, core, jnp.maximum(end_best, mine))
-        with jax.named_scope("w_near_too"):
-            arrived(NEAR_TOO, *near_too)
-        corner_near = scores(operand(corner), operand((chip, hub - 1)))
-        give(hub + 1, far_col, core, turn_max(jnp.maximum(fold(corner_end), fold(corner_near))))
-        near_mine, near_other = split(down_max(corner_near))
-        give(hub - 1, col, far_core, near_other)
-        hub_scores = scores(operand(near), operand((chip, hub)))
-        near_best = turn_max(jnp.maximum(folded_ref[row_count:left_size], fold(hub_scores)))
-        give(hub - 1, col, core, jnp.maximum(near_best, near_mine))
-        mine, other = split(beside_best)
-        give(hub, far_col, far_core, other)
-        beside_turned = jnp.maximum(beside_early, turn_max(folded_ref[left_size:]))
-        give(hub, far_col, core, jnp.maximum(beside_turned, mine))
-        hub_mine, hub_other = split(jnp.maximum(hub_best, down_max(hub_scores)))
-        give(hub, col, far_core, hub_other)
-        best_ref[0:1] = hub_mine
-        with jax.named_scope("w_sent"):
-            pass
+                send(CORNER_TOO, part, *corner, sibling_device, 1)
+            for part in range(CHUNKS):
+                with jax.named_scope("w_near%d" % part):
+                    pass_near(part)
+            with jax.named_scope("w_too"):
+                arrived(BESIDE_TOO, *beside_too)
+                arrived(END_TOO, *end_too)
+                arrived(CORNER_TOO, *corner_too)
+            left = operand(end, near)
+            near_outer = scores(operand(near), operand(outers))
+            left_corner = scores(left, operand((far_chip, hub + 1)))
+            give_outers(near_outer)
+            mine, other = split(down_max(left_corner))
+            give(hub + 1, far_col, far_core, other)
+            give(hub + 1, far_col, core, mine)
+            left_beside = scores(left, operand(besides))
+            near_end = scores(operand(near), operand(ends))
+            left_folded = jnp.maximum(fold(left_corner), fold(left_beside))
+            give_ends(down_max(near_end), left_folded[:row_count])
+            hub_scores = scores(operand(near), hubs)
+            near_folded = jnp.maximum(
+                jnp.maximum(fold(near_end), fold(near_outer)),
+                jnp.maximum(left_folded[row_count:], fold(hub_scores)),
+            )
+            give(hub - 1, col, core, turn_max(near_folded))
+            give_besides(down_max(left_beside))
+            give_hubs(hub_scores)
+
         sent(4, 2)
         sent(1, 4)
 

time: 20.3 us -> 20 us (0.985)
  Pallas kernels: 19.7 us -> 19.3 us
    pallas_call x1, Pallas kernels: 19.7 us -> 19.3 us  [meet_body(): pl.pallas_call(meet_kernel, out_shape=pltpu.VMEM((1, row_count), jnp.floa...]
where the time goes in v4:
time: 20 us; the launch traced here: 19.8 us
  Pallas kernels  19.3 us (96%)
  local copies, waits for them, and re-layouts  0.51 us (3%)
    pallas_call x1, Pallas kernels, meet_body(): pl.pallas_call(meet_kernel, out_shape=pltpu.VMEM((1, row_count), jnp.floa...  19.3 us
    unnamed x1, local copies, waits for them, and re-layouts  0.51 us

profile of v4, /device:TPU:0, one launch (start us, length us, event | category | flops | bytes accessed | tf_op | source)
XLA Modules:
  0.0 19.8 jit_solution(2923879858208151993)
XLA Ops:
  0.0 19.3 %scores.1 = f32[1,128]{1,0:T(1,128)S(1)} custom-call(bf16[128,2,1024]{2,1,0:T(2,128)(2,1)} %states_hbm.1, s32[1,128]{1,0:T(1,128)} %bitcast.6, s32[1,128]{1,0:T(1,128)} %bitcast.7, bf16[1024,1024]{1,0:T(8,128)(2,1)} %weight_hbm.1, f32[1,1024]{1,0:T(1,128)} %bitcast.5), custom_call_target="tpu_custom_call" | custom-call | tf_op jit(solution)/shard_map/scores/pallas_call | solution.py:784
  19.3 0.5 %copy.7 = f32[128]{0:T(128)} copy(f32[128]{0:T(128)S(1)} %bitcast.4) | data formatting | bytes 1024

commit v5 on v4

--- a/solution.py
+++ b/solution.py
@@ -86,8 +86,9 @@
 KEPT = 4
 ROUND = 1
 SAME = 4.0
-SIBLING, CORNER, NEAR_TOO, END_TOO, OUTER_TOO, BESIDE_TOO, CORNER_TOO, AFTER = range(8)
-ACROSS, OUTER, NEAR, END = (AFTER + 1 + CHUNKS * at for at in range(4))
+SIBLING, CORNER, NEAR_TOO, END_TOO, OUTER_TOO, BESIDE_TOO = range(6)
+AFTER, CORNER_TOO, WHOLE = CORNER, NEAR_TOO, BESIDE_TOO
+ACROSS, OUTER, NEAR, END = (WHOLE + 1 + CHUNKS * at for at in range(4))
 FLOWS = END + CHUNKS
 
 
@@ -107,12 +108,8 @@
     marks_ref,
     detour_ref,
     best_ref,
-    folded_ref,
     given_ref,
     taken_ref,
-    small_sem,
-    states_sem,
-    weight_sem,
     block_send,
     block_recv,
     detour_recv,
@@ -152,10 +149,10 @@
     me = spot(line, row)
     sibling_device = device(row, col, far_core)
 
-    states_copy = pltpu.make_async_copy(states_hbm, states_ref, states_sem)
+    states_copy = pltpu.make_async_copy(states_hbm, states_ref, block_send.at[3])
     states_copy.start()
     small_copies = [
-        pltpu.make_async_copy(source, held, small_sem.at[position])
+        pltpu.make_async_copy(source, held, block_send.at[position])
         for position, (source, held) in enumerate(
             [(lengths_hbm, lengths_ref), (ids_hbm, ids_ref.at[me]), (bias_hbm, bias_ref)]
         )
@@ -167,7 +164,7 @@
         pltpu.make_async_copy(
             weight_hbm.at[pl.ds(at * slab, slab)],
             weight_ref.at[pl.ds(at * slab, slab)],
-            weight_sem.at[at],
+            best_send if at else block_send.at[4],
         )
         for at in range(SLABS)
     ]
@@ -252,7 +249,7 @@
             src_ref=rows,
             dst_ref=rows,
             send_sem=block_send.at[lane],
-            recv_sem=block_recv.at[flow if flow <= AFTER else flow + part],
+            recv_sem=block_recv.at[flow if flow <= WHOLE else flow + part],
             device_id=where,
             device_id_type=pl.DeviceIdType.MESH,
         ).start()
@@ -796,12 +793,8 @@
             pltpu.VMEM((lines, ROWS, row_count, row_count), jnp.bfloat16),
             pltpu.VMEM((row_count, feat_dim), jnp.bfloat16),
             pltpu.VMEM((2, row_count), jnp.float32),
-            pltpu.VMEM((3 * row_count, row_count), jnp.float32),
             pltpu.VMEM((lines * ROWS, 1, row_count), jnp.float32),
             pltpu.VMEM((lines * ROWS, 1, row_count), jnp.float32),
-            pltpu.SemaphoreType.DMA((3,)),
-            pltpu.SemaphoreType.DMA,
-            pltpu.SemaphoreType.DMA((SLABS,)),
             pltpu.SemaphoreType.DMA((5,)),
             pltpu.SemaphoreType.DMA((FLOWS,)),
             pltpu.SemaphoreType.DMA((CHUNKS,)),

time: 20 us -> 19.9 us (level)
  no operation moved by 1% of the time
where the time goes in v5:
time: 19.9 us; the launch traced here: 19.7 us
  Pallas kernels  19.2 us (96%)
  local copies, waits for them, and re-layouts  0.51 us (3%)
    pallas_call x1, Pallas kernels, meet_body(): pl.pallas_call(meet_kernel, out_shape=pltpu.VMEM((1, row_count), jnp.floa...  19.2 us
    unnamed x1, local copies, waits for them, and re-layouts  0.51 us

profile of v5, /device:TPU:0, one launch (start us, length us, event | category | flops | bytes accessed | tf_op | source)
XLA Modules:
  0.0 19.7 jit_solution(15860602731637311719)
XLA Ops:
  0.0 19.2 %scores.1 = f32[1,128]{1,0:T(1,128)S(1)} custom-call(bf16[128,2,1024]{2,1,0:T(2,128)(2,1)} %states_hbm.1, s32[1,128]{1,0:T(1,128)} %bitcast.6, s32[1,128]{1,0:T(1,128)} %bitcast.7, bf16[1024,1024]{1,0:T(8,128)(2,1)} %weight_hbm.1, f32[1,1024]{1,0:T(1,128)} %bitcast.5), custom_call_target="tpu_custom_call" | custom-call | tf_op jit(solution)/shard_map/scores/pallas_call | solution.py:781
  19.2 0.5 %copy.7 = f32[128]{0:T(128)} copy(f32[128]{0:T(128)S(1)} %bitcast.4) | data formatting | bytes 1024

commit v6 on v5

--- a/solution.py
+++ b/solution.py
@@ -83,7 +83,6 @@
 CORES = 2
 CHUNKS = 4
 SLABS = 2
-KEPT = 4
 ROUND = 1
 SAME = 4.0
 SIBLING, CORNER, NEAR_TOO, END_TOO, OUTER_TOO, BESIDE_TOO = range(6)
@@ -457,37 +456,53 @@
     for part in range(CHUNKS):
         send(SIBLING, part, line, row, sibling_device, 4)
 
-    def send_across():
-        for part in range(CHUNKS):
+    def send_across(*parts):
+        for part in parts:
             send(ACROSS, part, line, row, device(row, far_col, core), 4)
 
     later = (row > hub) & (core == 1)
 
     @pl.when(jnp.logical_not(later))
     def _():
-        send_across()
+        send_across(*range(CHUNKS))
+
+    @pl.when(later)
+    def _():
+        send_across(CHUNKS - 1)
 
     mark(line, row)
 
     @pl.when(later)
     def _():
         sent(0, 1)
-        send_across()
+        send_across(*range(CHUNKS - 1))
 
     @pl.when(row != hub)
     def _():
-        for part in range(CHUNKS):
-            arrive(ACROSS, part, across_line, row)
-
-            @pl.when(row == 1)
-            def _():
-                send(AFTER, part, across_line, row, device(0, col, core), 1)
-
-            if part < KEPT:
-
-                @pl.when((row > hub) & (core == 0))
+        @pl.when(row < hub)
+        def _():
+            for part in range(CHUNKS):
+                arrive(ACROSS, part, across_line, row)
+
+                @pl.when(row == 1)
                 def _():
-                    send(CORNER, part, across_line, row, device(hub, col, core), 1)
+                    send(AFTER, part, across_line, row, device(0, col, core), 1)
+
+        @pl.when(row > hub)
+        def _():
+            @pl.when(core == 0)
+            def _():
+                for part in range(CHUNKS):
+                    arrive(ACROSS, part, across_line, row)
+                    if part:
+                        send(CORNER, part, across_line, row, device(hub, col, core), 1)
+
+            @pl.when(core == 1)
+            def _():
+                for part in (CHUNKS - 1, *range(CHUNKS - 1)):
+                    arrive(ACROSS, part, across_line, row)
+                    if part == CHUNKS - 1:
+                        send(CORNER, part, across_line, row, device(hub, col, core), 1)
 
         arrived(SIBLING, sibling_line, row)
 
@@ -555,7 +570,11 @@
 
             @pl.when(core == 0)
             def _():
-                sent_parts(1, KEPT)
+                sent_parts(1, CHUNKS - 1)
+
+            @pl.when(core == 1)
+            def _():
+                sent_parts(1, 1)
 
             @pl.when(group == 0)
             def _():
@@ -588,9 +607,11 @@
             arrive(OUTER, part, *outer)
             send(OUTER_TOO, part, *outer, sibling_device, 1)
 
-            @pl.when(True if part >= KEPT else core == 1)
-            def _():
-                send(CORNER, part, *outer, device(hub, far_col, core), 2)
+            if part < CHUNKS - 1:
+
+                @pl.when(core == 1 if part else core >= 0)
+                def _():
+                    send(CORNER, part, *outer, device(hub, far_col, core), 2)
 
         def pass_near(part):
             arrive(NEAR, part, *near)
@@ -757,12 +778,12 @@
 
         @pl.when(core == 1)
         def _():
-            sent(2, 1)
+            sent_parts(2, CHUNKS - 1)
             sent(3, 1)
 
         @pl.when(core == 0)
         def _():
-            pass
+            sent_parts(2, 1)
 
         @pl.when((core == 0) & passing)
         def _():

time: 19.9 us -> 19.9 us (level)
  no operation moved by 1% of the time
where the time goes in v6:
time: 19.9 us; the launch traced here: 19.7 us
  Pallas kernels  19.2 us (96%)
  local copies, waits for them, and re-layouts  0.51 us (3%)
    pallas_call x1, Pallas kernels, meet_body(): pl.pallas_call(meet_kernel, out_shape=pltpu.VMEM((1, row_count), jnp.floa...  19.2 us
    unnamed x1, local copies, waits for them, and re-layouts  0.51 us

profile of v6, /device:TPU:0, one launch (start us, length us, event | category | flops | bytes accessed | tf_op | source)
XLA Modules:
  0.0 19.7 jit_solution(1823384698482188792)
XLA Ops:
  0.0 19.2 %scores.1 = f32[1,128]{1,0:T(1,128)S(1)} custom-call(bf16[128,2,1024]{2,1,0:T(2,128)(2,1)} %states_hbm.1, s32[1,128]{1,0:T(1,128)} %bitcast.6, s32[1,128]{1,0:T(1,128)} %bitcast.7, bf16[1024,1024]{1,0:T(8,128)(2,1)} %weight_hbm.1, f32[1,1024]{1,0:T(1,128)} %bitcast.5), custom_call_target="tpu_custom_call" | custom-call | tf_op jit(solution)/shard_map/scores/pallas_call | solution.py:802
  19.2 0.5 %copy.7 = f32[128]{0:T(128)} copy(f32[128]{0:T(128)S(1)} %bitcast.4) | data formatting | bytes 1024
